TPU v7x, 32 devices: a whole 2x2x4 slice. The times are simulated.
32 devices in a mesh: blk: 4 (over y, core), order: 8 (over z, x).
Axes of the slice: x: 2, y: 2, z: 4, core: 2. Of those that a mesh axis runs over, the one named last changes fastest.
Arguments:
- sky_maps: float32 [16, 64, 8192], P(None, ('blk', 'order')), may hold values from -6 to 6
- wigner_d: bfloat16 [64, 1536, 2048], P(None, 'blk', 'order'), may hold values from -0.75 to 0.75
- order_of_slot: int32 [2048], replicated, may hold values from 0 to 2047, each once
- kernel: float32 [8, 2, 1536], P(None, None, 'blk'), may hold values from -6 to 6
Outputs:
- wavelet_coef: bfloat16 [8, 16, 2, 1536, 2048], P(None, None, None, 'blk', 'order')
Inputs may be any that keep to these rules, and one draw needn't show every extreme that they name: `order_of_slot`: every order appears in exactly one slot.
All inputs are finite; a program needn't handle non-finite values.
Results may differ from a plain program's by a relative error of at most 0.0049.
Values may be sent and summed in bfloat16 or wider, within the bound.
No kernel may reach another device: no remote copies, remote signals or barrier semaphores. Data moves between devices by JAX's collectives and lax.ppermute only.
A program may use at most 192 MiB of HBM per device.

v0:
```python
import math
import jax
import jax.numpy as jnp
from jax import lax
from jax.sharding import PartitionSpec as P

DEG_LO = 512
HIGHEST = lax.Precision.HIGHEST
RADIX = 128


def cycle_spectrum(sky_maps, orders):
    maps_count = sky_maps.shape[0]
    cycle_count = sky_maps.shape[1]
    samples = sky_maps.shape[2]
    outer_len = samples // RADIX
    order_blocks = orders // RADIX
    values = sky_maps.reshape(maps_count, cycle_count, RADIX, outer_len)
    inner_idx = jnp.arange(RADIX, dtype=jnp.int32)
    outer_idx = jnp.arange(outer_len, dtype=jnp.int32)
    block_idx = jnp.arange(order_blocks, dtype=jnp.int32)
    inner_angle = (
        2.0
        * math.pi
        / RADIX
        * (inner_idx[:, None] * inner_idx[None, :] % RADIX).astype(jnp.float32)
    )
    inner_re = jnp.einsum("abkj,km->abjm", values, jnp.cos(inner_angle), precision=HIGHEST)
    inner_im = -jnp.einsum("abkj,km->abjm", values, jnp.sin(inner_angle), precision=HIGHEST)
    twist_angle = (
        2.0 * math.pi / samples * (outer_idx[:, None] * inner_idx[None, :]).astype(jnp.float32)
    )
    twist_cos = jnp.cos(twist_angle)
    twist_sin = jnp.sin(twist_angle)
    turned_re = inner_re * twist_cos + inner_im * twist_sin
    turned_im = inner_im * twist_cos - inner_re * twist_sin
    outer_angle = (
        2.0
        * math.pi
        / outer_len
        * (block_idx[:, None] * outer_idx[None, :] % outer_len).astype(jnp.float32)
    )
    outer_cos = jnp.cos(outer_angle)
    outer_sin = jnp.sin(outer_angle)
    final_re = jnp.einsum("abjm,ij->abim", turned_re, outer_cos, precision=HIGHEST) + jnp.einsum(
        "abjm,ij->abim", turned_im, outer_sin, precision=HIGHEST
    )
    final_im = jnp.einsum("abjm,ij->abim", turned_im, outer_cos, precision=HIGHEST) - jnp.einsum(
        "abjm,ij->abim", turned_re, outer_sin, precision=HIGHEST
    )
    factor = 1.0 / math.sqrt(samples)
    stacked = jnp.stack(
        [
            final_re.reshape(maps_count, cycle_count, orders),
            final_im.reshape(maps_count, cycle_count, orders),
        ],
        axis=0,
    )
    return (stacked * factor).astype(jnp.bfloat16)


def add_cycles(piece, table):
    term = jnp.einsum("mrcs,rjs->mcjs", piece, table, preferred_element_type=jnp.float32)
    return term


def local(sky_maps, wigner_d, order_of_slot, kernel):
    orders = order_of_slot.shape[0]
    deg_count = wigner_d.shape[1]
    slot_count = wigner_d.shape[2]
    maps_count = sky_maps.shape[0]
    cycle_count = sky_maps.shape[1]
    groups = lax.axis_size("order")
    cycle_groups = lax.axis_size("blk")
    spectrum = cycle_spectrum(sky_maps, orders)
    slot_table = order_of_slot.reshape(groups, slot_count)
    order_ids = jnp.arange(orders, dtype=jnp.int32)
    one_hot = (order_ids[:, None, None] == slot_table[None, :, :]).astype(jnp.bfloat16)
    by_owner = jnp.einsum(
        "cmro,ogs->mgrcs", spectrum, one_hot, preferred_element_type=jnp.float32
    ).astype(jnp.bfloat16)
    copies = jnp.broadcast_to(
        by_owner[:, None], (maps_count, cycle_groups, groups, cycle_count, 2, slot_count)
    )
    copies = copies.reshape(maps_count, cycle_groups * groups * cycle_count, 2, slot_count)
    every_cycle = lax.all_to_all(copies, ("blk", "order"), split_axis=1, concat_axis=1, tiled=True)
    harmonic = add_cycles(every_cycle, wigner_d)
    my_orders = lax.dynamic_slice_in_dim(
        order_of_slot, lax.axis_index("order") * slot_count, slot_count, 0
    )
    degree = DEG_LO + lax.axis_index("blk") * deg_count + jnp.arange(deg_count, dtype=jnp.int32)
    live = degree[:, None] >= my_orders[None, :]
    real_part = jnp.where(live[None], harmonic[:, 0], 0.0)[None, :, None]
    imag_part = jnp.where(live[None], harmonic[:, 1], 0.0)[None, :, None]
    kern_re = kernel[:, 0, :]
    kern_im = kernel[:, 1, :]
    first = jnp.stack([kern_re, -kern_im], axis=1)[:, None, :, :, None]
    second = jnp.stack([kern_im, kern_re], axis=1)[:, None, :, :, None]
    return (real_part * first + imag_part * second).astype(jnp.bfloat16)


def solution(mesh):
    return jax.shard_map(
        local,
        mesh=mesh,
        in_specs=(
            P(None, ("blk", "order"), None),
            P(None, "blk", "order"),
            P(),
            P(None, None, "blk"),
        ),
        out_specs=P(None, None, None, "blk", "order"),
        check_vma=False,
    )
```

profile of v0, /device:TPU:0, one launch (start us, length us, event | category | flops | bytes accessed | tf_op | source)
XLA Modules:
  0.0 104.0 jit_solution(6579013343517247745)
XLA Ops:
  0.0 0.1 fusion.31
  0.1 2.3 %reshape.86 = f32[16,2,128,64]{3,2,1,0:T(8,128)S(1)} reshape(f32[16,2,8192]{2,1,0:T(2,128)} %param.4) | data formatting | bytes 2097152 | tf_op jit(solution)/shard_map/reshape | solution.py:18
  2.4 0.0 copy-start
  2.5 1.3 %copy-done = f32[16,2,128,64]{3,2,1,0:T(8,128)} copy-done((f32[16,2,128,64]{3,2,1,0:T(8,128)}, f32[16,2,128,64]{3,2,1,0:T(8,128)S(1)}, u32[]{:S(2)}) %copy-start) | copy-done | bytes 1048600
  3.8 0.0 copy-start.2
  3.8 3.5 %convolution_bitcast_fusion.1 = f32[16,2,64,128]{3,2,1,0:T(8,128)S(1)} fusion(f32[16,2,128,64]{3,2,1,0:T(8,128)S(1)} %reshape.86), kind=kOutput, calls=%fused_computation.12 | convolution fusion | flops 402882560 | bytes 2097152 | tf_op jit(solution)/shard_map/abkj,km->abjm/dot_general | solution.py:28
  7.3 5.1 %fusion.6 = f32[16,2,64,128]{3,2,1,0:T(8,128)S(1)} fusion(f32[16,2,128,64]{3,2,1,0:T(8,128)} %copy-done), kind=kOutput, calls=%fused_computation.11 | convolution fusion | flops 403144704 | bytes 2097152 | tf_op jit(solution)/shard_map/abkj,km->abjm/dot_general | solution.py:29
  12.3 0.7 fusion.17
  13.1 0.7 fusion.16
  13.9 0.0 copy-done.2
  13.9 0.8 fusion.10
  14.6 0.1 stack_reshape.7
  14.8 0.2 copy.29
  14.9 0.8 fusion.11
  15.7 0.1 stack_reshape.6
  15.9 0.2 copy.28
  16.0 3.2 %fusion.12 = bf16[16,8,2,2,256]{4,0,2,3,1:T(8,128)(2,1)S(1)} fusion(s32[8,256]{1,0:T(8,128)S(1)} %eq.20, f32[1,16,2,2048]{3,1,2,0:T(8,128)S(1)} %copy.29, f32[1,16,2,2048]{3,1,2,0:T(8,128)S(1)} %copy.28), kind=kOutput, calls=%fused_computation.18 | convolution fusion | flops 541589504 | bytes 794624 | tf_op jit(solution)/shard_map/cmro,ogs->mgrcs/dot_general | solution.py:79
  19.3 1.1 %broadcast_in_dim.15 = bf16[16,4,8,2,2,256]{5,0,4,3,2,1:T(8,128)(2,1)} broadcast(bf16[16,8,2,2,256]{4,0,3,2,1:T(8,128)(2,1)S(1)} %copy.30), dimensions={0,2,3,4,5} | broadcast | bytes 1310720 | tf_op jit(solution)/shard_map/broadcast_in_dim | solution.py:82
  20.4 7.3 %all-to-all-start = ((bf16[16,64,2,256]{3,0,2,1:T(8,128)(2,1)}), bf16[16,64,2,256]{3,0,2,1:T(8,128)(2,1)S(1)}, u32[]{:S(2)}, u32[]{:S(2)}) async-start(bf16[16,64,2,256]{3,0,2,1:T(8,128)(2,1)} %bitcast.18), calls=%async_computation | async-start | bytes 2097152 | tf_op jit(solution)/shard_map/all_to_all | solution.py:86
  27.7 0.1 dynamic_slice.3
  27.8 0.0 copy-start.1
  27.8 16.5 %copy.43 = bf16[64,384,256,1]{1,0,3,2:T(8,128)(2,1)} copy(bf16[64,384,256,1]{2,1,0,3:T(8,128)(2,1)} %bitcast.68) | data formatting | bytes 25165824 | tf_op args[1]
  44.3 0.0 copy-done.1
  44.4 0.1 broadcast_compare_fusion
  44.5 10.8 %all-to-all-done = bf16[16,64,2,256]{3,0,2,1:T(8,128)(2,1)S(1)} async-done(((bf16[16,64,2,256]{3,0,2,1:T(8,128)(2,1)}), bf16[16,64,2,256]{3,0,2,1:T(8,128)(2,1)S(1)}, u32[]{:S(2)}, u32[]{:S(2)}) %all-to-all-start) | async-done | bytes 1048608 | tf_op jit(solution)/shard_map/all_to_all | solution.py:86
  55.3 3.5 %copy.31 = bf16[16,64,2,256]{1,0,2,3:T(8,128)(2,1)S(1)} copy(bf16[16,64,2,256]{3,0,2,1:T(8,128)(2,1)S(1)} %all-to-all-done) | data formatting | bytes 2097152 | tf_op jit(solution)/shard_map/all_to_all | solution.py:86
  58.8 5.9 %convolution_bitcast_fusion = f32[16,2,384,256]{2,0,1,3:T(8,128)S(1)} fusion(bf16[16,64,2,256]{1,0,2,3:T(8,128)(2,1)S(1)} %copy.31, bf16[64,384,256,1]{1,0,3,2:T(8,128)(2,1)} %copy.43), kind=kOutput, calls=%fused_computation.9 | convolution fusion | flops 402653184 | bytes 26214400 | tf_op jit(solution)/shard_map/mrcs,rjs->mcjs/dot_general | solution.py:63
  64.7 5.4 %fusion.5 = (f32[16,384,256]{1,0,2:T(8,128)}, f32[16,384,256]{1,0,2:T(8,128)}) fusion(f32[16,2,384,256]{2,0,1,3:T(8,128)S(1)} %convolution_bitcast_fusion, pred[384,256]{0,1:T(8,128)(4,1)S(1)} %broadcast_compare_fusion), kind=kLoop, calls=%fused_computation.8 | loop fusion | flops 3145728 | bytes 25264128 | tf_op jit(solution)/shard_map/jit(_where)/select_n | solution.py:93
  70.1 6.6 %copy.34 = f32[16,384,256]{2,1,0:T(8,128)} copy(f32[16,384,256]{1,0,2:T(8,128)} %get-tuple-element.5) | data formatting | bytes 12582912 | tf_op jit(solution)/shard_map/jit(_where)/select_n | solution.py:93
  76.7 6.6 %copy.35 = f32[16,384,256]{2,1,0:T(8,128)} copy(f32[16,384,256]{1,0,2:T(8,128)} %get-tuple-element.6) | data formatting | bytes 12582912 | tf_op jit(solution)/shard_map/jit(_where)/select_n | solution.py:94
  83.3 20.6 %add_convert_fusion = bf16[8,16,2,384,256]{4,3,2,1,0:T(8,128)(2,1)} fusion(f32[8,2,384]{2,1,0:T(2,128)S(1)} %get-tuple-element.11, f32[16,384,256]{2,1,0:T(8,128)} %copy.35, f32[8,2,384]{2,1,0:T(2,128)S(1)} %get-tuple-element.10, f32[16,384,256]{2,1,0:T(8,128)} %copy.34), kind=kLoop, calls=%fused_computation | loop fusion | flops 100663296 | bytes 62963712 | tf_op jit(solution)/shard_map/convert_element_type | solution.py:99
  (5 shorter events, 0.1 us)
Async XLA Ops:
  2.4 1.3 %copy-start = (f32[16,2,128,64]{3,2,1,0:T(8,128)}, f32[16,2,128,64]{3,2,1,0:T(8,128)S(1)}, u32[]{:S(2)}) copy-start(f32[16,2,128,64]{3,2,1,0:T(8,128)S(1)} %reshape.86) | copy-start | bytes 3145732
  3.8 10.1 %copy-start.2 = (s32[2048]{0:T(1024)S(1)}, s32[2048]{0:T(1024)}, u32[]{:S(2)}) copy-start(s32[2048]{0:T(1024)} %param.6) | copy-start | bytes 24580
  20.4 34.9 %all-to-all-start = ((bf16[16,64,2,256]{3,0,2,1:T(8,128)(2,1)}), bf16[16,64,2,256]{3,0,2,1:T(8,128)(2,1)S(1)}, u32[]{:S(2)}, u32[]{:S(2)}) async-start(bf16[16,64,2,256]{3,0,2,1:T(8,128)(2,1)} %bitcast.18), calls=%async_computation | async-start | bytes 2097152 | tf_op jit(solution)/shard_map/all_to_all | solution.py:86
  27.8 16.5 %copy-start.1 = (f32[8,2,384]{2,1,0:T(2,128)S(1)}, f32[8,2,384]{2,1,0:T(2,128)}, u32[]{:S(2)}) copy-start(f32[8,2,384]{2,1,0:T(2,128)} %param.7) | copy-start | bytes 73732
where the time goes:
time: 105 us; the launch traced here: 104 us
  local copies, waits for them, and re-layouts  38.7 us (37%)
  other arithmetic  26.3 us (25%)
  matrix products  20.6 us (20%)
  waiting for transfers between devices  10.8 us (10%)
  starting transfers between devices  7.3 us (7%)
    convert_element_type x1, other arithmetic, local(): return (real_part * first + imag_part * second).astype(jnp.bfloat16)  20.6 us
    unnamed x7, local copies, waits for them, and re-layouts  17.8 us
    all_to_all x1, waiting for transfers between devices, local(): lax.all_to_all(copies, ('blk', 'order'), split_axis=1, concat_axis=1, til...  10.8 us
    all_to_all x1, starting transfers between devices, local(): lax.all_to_all(copies, ('blk', 'order'), split_axis=1, concat_axis=1, til...  7.3 us
    select_n x1, local copies, waits for them, and re-layouts, local(): real_part = jnp.where(live[None], harmonic[:, 0], 0.0)[None, :, None]  6.61 us
    select_n x1, local copies, waits for them, and re-layouts, local(): imag_part = jnp.where(live[None], harmonic[:, 1], 0.0)[None, :, None]  6.6 us
    dot_general x1, matrix products, add_cycles(): jnp.einsum('mrcs,rjs->mcjs', piece, table, preferred_element_type=jnp.flo...  5.86 us
    select_n x1, other arithmetic, local(): real_part = jnp.where(live[None], harmonic[:, 0], 0.0)[None, :, None]  5.4 us
  transfers between devices with their start and end apart: 1, of which 1 were waited for; matrix products, arithmetic and copies ran while one was open for 16% of the time, Pallas kernels for 0%

commit v1 on v0

--- a/solution.py
+++ b/solution.py
@@ -83,7 +83,10 @@
         by_owner[:, None], (maps_count, cycle_groups, groups, cycle_count, 2, slot_count)
     )
     copies = copies.reshape(maps_count, cycle_groups * groups * cycle_count, 2, slot_count)
-    every_cycle = lax.all_to_all(copies, ("blk", "order"), split_axis=1, concat_axis=1, tiled=True)
+    n_dev = lax.axis_size(("blk", "order"))
+    blocks = jnp.stack(jnp.split(copies, n_dev, axis=1), axis=0)
+    blocks = lax.all_to_all(blocks, ("blk", "order"), split_axis=0, concat_axis=0)
+    every_cycle = jnp.concatenate(blocks, axis=1)
     harmonic = add_cycles(every_cycle, wigner_d)
     my_orders = lax.dynamic_slice_in_dim(
         order_of_slot, lax.axis_index("order") * slot_count, slot_count, 0

time: 105 us -> 123 us (1.17)
  local copies, waits for them, and re-layouts: 38.7 us -> 57.3 us
    unnamed x7 -> x38, local copies, waits for them, and re-layouts: 17.8 us -> 36.8 us
    all_to_all x1 -> x0, local copies, waits for them, and re-layouts: 3.54 us -> none  [local(): lax.all_to_all(copies, ('blk', 'order'), split_axis=1, concat_axis=1, til...]
    reshape x0 -> x1, local copies, waits for them, and re-layouts: none -> 3.54 us  [local(): every_cycle = jnp.concatenate(blocks, axis=1)]
  transfers between devices with their start and end apart: 1 -> 1, of which waited for: 1 -> 1; matrix products, arithmetic and copies ran while one was open for 16% -> 14% of each run, Pallas kernels for 0% -> 0%
where the time goes in v1:
time: 123 us
  local copies, waits for them, and re-layouts  57.3 us (47%)
  other arithmetic  26.3 us (21%)
  matrix products  20.6 us (17%)
  waiting for transfers between devices  10.8 us (9%)
  starting transfers between devices  7.3 us (6%)
    unnamed x38, local copies, waits for them, and re-layouts  36.8 us
    convert_element_type x1, other arithmetic, local(): return (real_part * first + imag_part * second).astype(jnp.bfloat16)  20.6 us
    all_to_all x1, waiting for transfers between devices, local(): lax.all_to_all(blocks, ('blk', 'order'), split_axis=0, concat_axis=0)  10.8 us
    all_to_all x1, starting transfers between devices, local(): lax.all_to_all(blocks, ('blk', 'order'), split_axis=0, concat_axis=0)  7.3 us
    select_n x1, local copies, waits for them, and re-layouts, local(): real_part = jnp.where(live[None], harmonic[:, 0], 0.0)[None, :, None]  6.61 us
    select_n x1, local copies, waits for them, and re-layouts, local(): imag_part = jnp.where(live[None], harmonic[:, 1], 0.0)[None, :, None]  6.6 us
    dot_general x1, matrix products, add_cycles(): jnp.einsum('mrcs,rjs->mcjs', piece, table, preferred_element_type=jnp.flo...  5.86 us
    select_n x1, other arithmetic, local(): real_part = jnp.where(live[None], harmonic[:, 0], 0.0)[None, :, None]  5.4 us
  transfers between devices with their start and end apart: 1, of which 1 were waited for; matrix products, arithmetic and copies ran while one was open for 14% of the time, Pallas kernels for 0%

profile of v1, /device:TPU:0, one launch (start us, length us, event | category | flops | bytes accessed | tf_op | source)
XLA Modules:
  0.0 122.7 jit_solution(16169933105190356941)
XLA Ops:
  0.1 2.3 %reshape.94 = f32[16,2,128,64]{3,2,1,0:T(8,128)S(1)} reshape(f32[16,2,8192]{2,1,0:T(2,128)} %param.4) | data formatting | bytes 2097152 | tf_op jit(solution)/shard_map/reshape | solution.py:18
  2.5 1.3 %copy-done = f32[16,2,128,64]{3,2,1,0:T(8,128)} copy-done((f32[16,2,128,64]{3,2,1,0:T(8,128)}, f32[16,2,128,64]{3,2,1,0:T(8,128)S(1)}, u32[]{:S(2)}) %copy-start) | copy-done | bytes 1048600
  3.8 3.5 %convolution_bitcast_fusion.1 = f32[16,2,64,128]{3,2,1,0:T(8,128)S(1)} fusion(f32[16,2,128,64]{3,2,1,0:T(8,128)S(1)} %reshape.94), kind=kOutput, calls=%fused_computation.12 | convolution fusion | flops 402882560 | bytes 2097152 | tf_op jit(solution)/shard_map/abkj,km->abjm/dot_general | solution.py:28
  7.3 5.1 %fusion.6 = f32[16,2,64,128]{3,2,1,0:T(8,128)S(1)} fusion(f32[16,2,128,64]{3,2,1,0:T(8,128)} %copy-done), kind=kOutput, calls=%fused_computation.11 | convolution fusion | flops 403144704 | bytes 2097152 | tf_op jit(solution)/shard_map/abkj,km->abjm/dot_general | solution.py:29
  12.3 0.7 fusion.17
  13.1 0.7 fusion.16
  13.9 0.8 fusion.10
  14.9 0.8 fusion.11
  16.0 3.2 %fusion.12 = bf16[16,8,2,2,256]{4,0,2,3,1:T(8,128)(2,1)S(1)} fusion(s32[8,256]{1,0:T(8,128)S(1)} %eq.20, f32[1,16,2,2048]{3,1,2,0:T(8,128)S(1)} %copy.49, f32[1,16,2,2048]{3,1,2,0:T(8,128)S(1)} %copy.48), kind=kOutput, calls=%fused_computation.18 | convolution fusion | flops 541589504 | bytes 794624 | tf_op jit(solution)/shard_map/cmro,ogs->mgrcs/dot_general | solution.py:79
  20.0 0.6 constant_dynamic-update-slice_fusion.30
  20.6 0.6 constant_dynamic-update-slice_fusion.29
  22.5 0.6 constant_dynamic-update-slice_fusion.26
  24.3 0.6 constant_dynamic-update-slice_fusion.23
  26.8 0.6 constant_dynamic-update-slice_fusion.19
  27.4 0.6 constant_dynamic-update-slice_fusion.18
  28.0 0.6 constant_dynamic-update-slice_fusion.17
  28.6 0.6 constant_dynamic-update-slice_fusion.16
  30.4 0.6 constant_dynamic-update-slice_fusion.13
  34.1 0.6 constant_dynamic-update-slice_fusion.7
  35.3 0.6 constant_dynamic-update-slice_fusion.5
  36.6 0.6 constant_dynamic-update-slice_fusion.3
  37.2 0.6 constant_dynamic-update-slice_fusion.2
  38.4 0.6 constant_dynamic-update-slice_fusion
  39.0 7.3 %all-to-all-start = ((bf16[32,16,2,2,256]{4,1,3,2,0:T(8,128)(2,1)}), bf16[32,16,2,2,256]{4,1,3,2,0:T(8,128)(2,1)S(1)}, u32[]{:S(2)}, u32[]{:S(2)}) async-start(bf16[32,16,2,2,256]{4,1,3,2,0:T(8,128)(2,1)} %constant_dynamic-update-slice_fusion), calls=%async_computation | async-start | bytes 2097152 | tf_op jit(solution)/shard_map/all_to_all | solution.py:88
  46.4 16.5 %copy.63 = bf16[64,384,256,1]{1,0,3,2:T(8,128)(2,1)} copy(bf16[64,384,256,1]{2,1,0,3:T(8,128)(2,1)} %bitcast.199) | data formatting | bytes 25165824 | tf_op args[1]
  63.2 10.8 %all-to-all-done = bf16[32,16,2,2,256]{4,1,3,2,0:T(8,128)(2,1)S(1)} async-done(((bf16[32,16,2,2,256]{4,1,3,2,0:T(8,128)(2,1)}), bf16[32,16,2,2,256]{4,1,3,2,0:T(8,128)(2,1)S(1)}, u32[]{:S(2)}, u32[]{:S(2)}) %all-to-all-start) | async-done | bytes 1048608 | tf_op jit(solution)/shard_map/all_to_all | solution.py:88
  73.9 3.5 %copy.51 = bf16[16,64,2,256]{1,0,2,3:T(8,128)(2,1)S(1)} copy(bf16[16,64,2,256]{3,0,2,1:T(8,128)(2,1)S(1)} %bitcast.232) | data formatting | bytes 2097152 | tf_op jit(solution)/shard_map/reshape | solution.py:89
  77.5 5.9 %convolution_bitcast_fusion = f32[16,2,384,256]{2,0,1,3:T(8,128)S(1)} fusion(bf16[16,64,2,256]{1,0,2,3:T(8,128)(2,1)S(1)} %copy.51, bf16[64,384,256,1]{1,0,3,2:T(8,128)(2,1)} %copy.63), kind=kOutput, calls=%fused_computation.9 | convolution fusion | flops 402653184 | bytes 26214400 | tf_op jit(solution)/shard_map/mrcs,rjs->mcjs/dot_general | solution.py:63
  83.3 5.4 %fusion.5 = (f32[16,384,256]{1,0,2:T(8,128)}, f32[16,384,256]{1,0,2:T(8,128)}) fusion(f32[16,2,384,256]{2,0,1,3:T(8,128)S(1)} %convolution_bitcast_fusion, pred[384,256]{0,1:T(8,128)(4,1)S(1)} %broadcast_compare_fusion), kind=kLoop, calls=%fused_computation.8 | loop fusion | flops 3145728 | bytes 25264128 | tf_op jit(solution)/shard_map/jit(_where)/select_n | solution.py:96
  88.7 6.6 %copy.54 = f32[16,384,256]{2,1,0:T(8,128)} copy(f32[16,384,256]{1,0,2:T(8,128)} %get-tuple-element.5) | data formatting | bytes 12582912 | tf_op jit(solution)/shard_map/jit(_where)/select_n | solution.py:96
  95.4 6.6 %copy.55 = f32[16,384,256]{2,1,0:T(8,128)} copy(f32[16,384,256]{1,0,2:T(8,128)} %get-tuple-element.6) | data formatting | bytes 12582912 | tf_op jit(solution)/shard_map/jit(_where)/select_n | solution.py:97
  102.0 20.6 %add_convert_fusion = bf16[8,16,2,384,256]{4,3,2,1,0:T(8,128)(2,1)} fusion(f32[8,2,384]{2,1,0:T(2,128)S(1)} %get-tuple-element.11, f32[16,384,256]{2,1,0:T(8,128)} %copy.55, f32[8,2,384]{2,1,0:T(2,128)S(1)} %get-tuple-element.10, f32[16,384,256]{2,1,0:T(8,128)} %copy.54), kind=kLoop, calls=%fused_computation | loop fusion | flops 100663296 | bytes 62963712 | tf_op jit(solution)/shard_map/convert_element_type | solution.py:102
  (36 shorter events, 12.1 us)
Async XLA Ops:
  2.4 1.3 %copy-start = (f32[16,2,128,64]{3,2,1,0:T(8,128)}, f32[16,2,128,64]{3,2,1,0:T(8,128)S(1)}, u32[]{:S(2)}) copy-start(f32[16,2,128,64]{3,2,1,0:T(8,128)S(1)} %reshape.94) | copy-start | bytes 3145732
  3.8 10.1 %copy-start.2 = (s32[2048]{0:T(1024)S(1)}, s32[2048]{0:T(1024)}, u32[]{:S(2)}) copy-start(s32[2048]{0:T(1024)} %param.6) | copy-start | bytes 24580
  39.0 34.9 %all-to-all-start = ((bf16[32,16,2,2,256]{4,1,3,2,0:T(8,128)(2,1)}), bf16[32,16,2,2,256]{4,1,3,2,0:T(8,128)(2,1)S(1)}, u32[]{:S(2)}, u32[]{:S(2)}) async-start(bf16[32,16,2,2,256]{4,1,3,2,0:T(8,128)(2,1)} %constant_dynamic-update-slice_fusion), calls=%async_computation | async-start | bytes 2097152 | tf_op jit(solution)/shard_map/all_to_all | solution.py:88
  46.4 16.5 %copy-start.1 = (f32[8,2,384]{2,1,0:T(2,128)S(1)}, f32[8,2,384]{2,1,0:T(2,128)}, u32[]{:S(2)}) copy-start(f32[8,2,384]{2,1,0:T(2,128)} %param.7) | copy-start | bytes 73732
